TPU v7x, 32 devices: a whole 2x2x4 slice. The times are simulated.
32 devices in a mesh: expert: 4 (over z), dp: 8 (over y, x, core).
Axes of the slice: x: 2, y: 2, z: 4, core: 2. Of those that a mesh axis runs over, the one named last changes fastest.
Arguments:
- grad_out: bfloat16 [4096, 2048], P(('expert', 'dp')), may hold values from -1.59375 to 1.59375
- slot_token: int32 [32, 8, 8], P(('expert', 'dp')), may hold values from 0 to 127, as said below
- hidden: bfloat16 [2048, 768], P(('expert', 'dp')), may hold values from -6 to 6
- slot_weight: float32 [32, 64], P(('expert', 'dp')), may hold values from 0.05 to 0.5
- counts: int32 [32, 8], P(('expert', 'dp')), may hold values from 0 to 8, as said below
- master_weight: bfloat16 [8, 768, 2048], P('expert', 'dp')
- moment1: bfloat16 [8, 768, 2048], P('expert', 'dp')
- moment2: bfloat16 [8, 768, 2048], P('expert', 'dp'), may hold values from 0.099609375 to 2
Outputs:
- new_weight: bfloat16 [8, 768, 2048], P('expert', 'dp')
Inputs may be any that keep to these rules, and one draw needn't show every extreme that they name: `slot_token`: within one device's block for one expert, the 8 slots name different tokens. `counts`: in every draw some expert has 8 live slots from every device.
All inputs are finite; a program needn't handle non-finite values.
Results may differ from a plain program's by a relative error of at most 0.0055.
Values may be sent and summed in bfloat16 or wider, within the bound.
A program may use at most 64 MiB of HBM per device.

v0:
```python
import jax
import jax.numpy as jnp
from jax import lax
from jax.sharding import PartitionSpec as P

learn_rate = 0.3
decay_rate = 0.01
adam_eps = 1e-06
norm_eps = 1e-06
bias_one = 1.0 - 0.9**10
bias_two = 1.0 - 0.999**10


def local(grad_out, slot_token, hidden, slot_weight, counts, master_weight, moment1, moment2):
    n_expert = lax.axis_size("expert")
    experts_here = master_weight.shape[0]
    capacity = slot_token.shape[2]
    width = grad_out.shape[1]
    depth = hidden.shape[1]
    weight = master_weight.astype(jnp.float32)
    first = moment1.astype(jnp.float32)
    second = moment2.astype(jnp.float32)
    weight_sq = jnp.sum(weight * weight, axis=(1, 2))
    weight_total = lax.psum(weight_sq, "dp")
    picked = jnp.take(grad_out, slot_token.reshape(-1), axis=0).reshape(
        n_expert, experts_here * capacity, width
    )
    arrived = lax.all_to_all(picked, "expert", split_axis=0, concat_axis=0, tiled=True)
    arrived = arrived.reshape(n_expert, experts_here, capacity, width)
    slot_ids = lax.broadcasted_iota(jnp.int32, (n_expert, experts_here, capacity), 2)
    is_live = slot_ids < counts.reshape(n_expert, experts_here)[:, :, None]
    mixing = jnp.where(is_live, slot_weight.reshape(n_expert, experts_here, capacity), 0.0).astype(
        jnp.bfloat16
    )
    scaled = (mixing.astype(jnp.float32)[..., None] * arrived.astype(jnp.float32)).astype(
        jnp.bfloat16
    )
    saved = hidden.reshape(n_expert, experts_here, capacity, depth)
    shares = []
    for j in range(experts_here):
        saved_rows = saved[:, j].reshape(-1, depth)
        scaled_rows = scaled[:, j].reshape(-1, width)
        term = jnp.dot(saved_rows.T, scaled_rows, preferred_element_type=jnp.float32)
        shares.append(
            lax.psum_scatter(
                term.astype(jnp.bfloat16).astype(jnp.float32).astype(jnp.bfloat16),
                "dp",
                scatter_dimension=0,
                tiled=True,
            ).astype(jnp.float32)
        )
    gradient = jnp.stack(shares)
    first_new = 0.9 * first + 0.1 * gradient
    second_new = 0.999 * second + 0.001 * gradient * gradient
    update = (
        first_new / bias_one / (jnp.sqrt(second_new / bias_two) + adam_eps) + decay_rate * weight
    )
    update_sq = jnp.sum(update * update, axis=(1, 2))
    update_total = lax.psum(update_sq, "dp")
    trust_ratio = jnp.sqrt(weight_total) / (jnp.sqrt(update_total) + norm_eps)
    fresh = weight - learn_rate * trust_ratio[:, None, None] * update
    return fresh.astype(jnp.bfloat16)


def solution(mesh):
    placed = (
        P(("expert", "dp"), None),
        P(("expert", "dp"), None, None),
        P(("expert", "dp"), None),
        P(("expert", "dp"), None),
        P(("expert", "dp"), None),
        P("expert", "dp", None),
        P("expert", "dp", None),
        P("expert", "dp", None),
    )
    return jax.shard_map(
        local, mesh=mesh, in_specs=placed, out_specs=P("expert", "dp", None), check_vma=False
    )
```

profile of v0, /device:TPU:0, one launch (start us, length us, event | category | flops | bytes accessed | tf_op | source)
XLA Modules:
  0.0 151.3 jit_solution(233067076570586812)
XLA Ops:
  6.5 0.0 copy-start
  6.5 0.8 reshape.83
  7.4 0.8 reshape.82
  8.2 0.0 copy-done
  8.2 0.0 copy-start.3
  8.2 0.0 copy-start.4
  8.2 0.0 copy-start.2
  8.2 0.7 gather_fusion
  8.9 0.8 broadcast_select_fusion
  9.7 6.3 %all-to-all-start = ((bf16[4,16,2048]{2,1,0:T(8,128)(2,1)}), bf16[4,16,2048]{2,1,0:T(8,128)(2,1)S(1)}, u32[]{:S(2)}, u32[]{:S(2)}) async-start(bf16[4,16,2048]{2,1,0:T(8,128)(2,1)} %broadcast_select_fusion), calls=%async_computation | async-start | bytes 524288 | tf_op jit(solution)/shard_map/all_to_all | solution.py:28
  16.1 0.0 reduce-scatter.9.cloned.1.call-start
  16.1 0.6 broadcast.63
  16.7 0.0 copy-done.3
  16.7 0.7 reduce.6
  17.4 0.1 reshape.81
  17.5 0.6 broadcast.64
  18.1 0.0 copy-done.4
  18.1 0.7 reduce.7
  18.8 0.1 lt.36
  18.9 0.1 fusion.14
  19.0 6.0 %all-to-all-done = bf16[4,16,2048]{2,1,0:T(8,128)(2,1)S(1)} async-done(((bf16[4,16,2048]{2,1,0:T(8,128)(2,1)}), bf16[4,16,2048]{2,1,0:T(8,128)(2,1)S(1)}, u32[]{:S(2)}, u32[]{:S(2)}) %all-to-all-start) | async-done | bytes 262176 | tf_op jit(solution)/shard_map/all_to_all | solution.py:28
  25.0 0.1 fusion.12
  25.1 0.0 copy-done.2
  25.1 2.7 %fusion.1 = bf16[768,2048]{0,1:T(8,128)(2,1)} fusion(bf16[4,2,8,2048]{3,2,0,1:T(8,128)(2,1)S(1)} %fusion.12, bf16[4,2,8,768]{3,2,1,0:T(8,128)(2,1)S(1)} %bitcast.43), kind=kOutput, calls=%fused_computation.4 | convolution fusion | flops 102236160 | bytes 3325952 | tf_op jit(solution)/shard_map/dot_general | solution.py:43
  27.9 4.8 %copy.38 = bf16[768,2048]{1,0:T(8,128)(2,1)} copy(bf16[768,2048]{0,1:T(8,128)(2,1)} %fusion.1) | data formatting | bytes 6291456
  32.6 0.0 reduce-scatter.9.cloned.1.call-update
  32.6 0.0 reduce-scatter.7.cloned.1.call-start
  32.7 2.7 %fusion = bf16[768,2048]{0,1:T(8,128)(2,1)} fusion(bf16[4,2,8,2048]{3,2,0,1:T(8,128)(2,1)S(1)} %fusion.12, bf16[4,2,8,768]{3,2,1,0:T(8,128)(2,1)S(1)} %bitcast.44), kind=kOutput, calls=%fused_computation.3 | convolution fusion | flops 102236160 | bytes 3325952 | tf_op jit(solution)/shard_map/dot_general | solution.py:43
  35.4 4.7 %copy.36 = bf16[768,2048]{1,0:T(8,128)(2,1)} copy(bf16[768,2048]{0,1:T(8,128)(2,1)} %fusion) | data formatting | bytes 6291456
  40.2 0.0 copy-start.1
  40.2 0.0 reduce-scatter.7.cloned.1.call-update
  40.2 37.7 %reduce-scatter.9.cloned.1.call-done = bf16[96,2048]{1,0:T(8,128)(2,1)} async-done(((bf16[768,2048]{1,0:T(8,128)(2,1)}), bf16[96,2048]{1,0:T(8,128)(2,1)}) %reduce-scatter.9.cloned.1.call-update) | async-done | bytes 393232 | tf_op jit(solution)/shard_map/reduce_scatter | solution.py:45
  77.9 49.5 %reduce-scatter.7.cloned.1.call-done = bf16[96,2048]{1,0:T(8,128)(2,1)} async-done(((bf16[768,2048]{1,0:T(8,128)(2,1)}), bf16[96,2048]{1,0:T(8,128)(2,1)}) %reduce-scatter.7.cloned.1.call-update) | async-done | bytes 393232 | tf_op jit(solution)/shard_map/reduce_scatter | solution.py:45
  127.4 0.0 copy-done.1
  127.4 3.4 %multiply_reduce_fusion = (f32[2]{0:T(128)S(1)}, f32[2,96,2048]{2,1,0:T(8,128)S(1)}, f32[2]{0:T(128)S(1)}) fusion(bf16[2,96,2048]{2,1,0:T(8,128)(2,1)S(1)} %copy-done.1, bf16[2,96,2048]{2,1,0:T(8,128)(2,1)} %param.15, bf16[1,96,2048]{2,1,0:T(8,128)(2,1)} %bitcast.41, bf16[1,96,2048]{2,1,0:T(8,128)(2,1)} %bitcast.42, bf16[2,96,2048]{2,1,0:T(8,128)(2,1)} %param.14), kind=kLoop, calls=%fused_computation.20 | loop fusion | flops 8650748 | bytes 4718608 | tf_op jit(solution)/shard_map/reduce_sum | solution.py:58
  130.8 12.5 %all-reduce = (f32[2]{0:T(128)S(1)}, f32[2]{0:T(128)S(1)}) all-reduce(f32[2]{0:T(128)S(1)} %get-tuple-element.7, f32[2]{0:T(128)S(1)} %get-tuple-element.9), channel_id=1, replica_groups=mesh['expert'=4,'dp'=8] {'dp'}, use_global_device_ids=true, to_apply=%region_5.6 | all-reduce | flops 4 | bytes 32 | tf_op jit(solution)/shard_map/psum | solution.py:59
  143.3 1.2 fusion.7
  (5 shorter events, 0.0 us)
Async XLA Ops:
  6.5 1.6 %copy-start = (bf16[128,2048]{1,0:T(8,128)(2,1)S(1)}, bf16[128,2048]{1,0:T(8,128)(2,1)}, u32[]{:S(2)}) copy-start(bf16[128,2048]{1,0:T(8,128)(2,1)} %param.8) | copy-start | bytes 1572868
  8.2 8.5 %copy-start.3 = (f32[1,64]{1,0:T(1,128)S(1)}, f32[1,64]{1,0:T(1,128)}, u32[]{:S(2)}) copy-start(f32[1,64]{1,0:T(1,128)} %param.11) | copy-start | bytes 772
  8.2 9.9 %copy-start.4 = (s32[1,8]{1,0:T(1,128)S(1)}, s32[1,8]{1,0:T(1,128)}, u32[]{:S(2)}) copy-start(s32[1,8]{1,0:T(1,128)} %param.12) | copy-start | bytes 100
  8.2 16.9 %copy-start.2 = (bf16[64,768]{1,0:T(8,128)(2,1)S(1)}, bf16[64,768]{1,0:T(8,128)(2,1)}, u32[]{:S(2)}) copy-start(bf16[64,768]{1,0:T(8,128)(2,1)} %param.10) | copy-start | bytes 294916
  9.7 15.3 %all-to-all-start = ((bf16[4,16,2048]{2,1,0:T(8,128)(2,1)}), bf16[4,16,2048]{2,1,0:T(8,128)(2,1)S(1)}, u32[]{:S(2)}, u32[]{:S(2)}) async-start(bf16[4,16,2048]{2,1,0:T(8,128)(2,1)} %broadcast_select_fusion), calls=%async_computation | async-start | bytes 524288 | tf_op jit(solution)/shard_map/all_to_all | solution.py:28
  16.1 61.8 %reduce-scatter.9.cloned.1.call-start = ((), (), s32[]{:S(2)}) async-start(), calls=%async_computation.4 | async-start | bytes 3538944 | tf_op jit(solution)/shard_map/reduce_scatter | solution.py:45
  32.6 94.7 %reduce-scatter.7.cloned.1.call-start = ((), (), s32[]{:S(2)}) async-start(), calls=%async_computation.3 | async-start | bytes 3538944 | tf_op jit(solution)/shard_map/reduce_scatter | solution.py:45
  40.2 87.2 %copy-start.1 = (bf16[2,96,2048]{2,1,0:T(8,128)(2,1)S(1)}, bf16[2,96,2048]{2,1,0:T(8,128)(2,1)}, u32[]{:S(2)}) copy-start(bf16[2,96,2048]{2,1,0:T(8,128)(2,1)} %param.13) | copy-start | bytes 2359300
Sparse Core Ops, SparseCore 0:
  32.8 45.1 reduce-scatter.8
  81.3 46.0 reduce-scatter.6
where the time goes:
time: 152 us; the launch traced here: 151 us
  waiting for transfers between devices  93.3 us (61%)
  between operations  13.5 us (9%)
  local copies, waits for them, and re-layouts  13.2 us (9%)
  blocking collectives  12.5 us (8%)
  other arithmetic  6.99 us (5%)
  starting transfers between devices  6.39 us (4%)
  matrix products  5.47 us (4%)
    reduce_scatter x2, waiting for transfers between devices, local(): lax.psum_scatter(term.astype(jnp.bfloat16).astype(jnp.float32).astype(jnp...  87.2 us
    psum x1, blocking collectives, local(): update_total = lax.psum(update_sq, 'dp')  12.5 us
    unnamed x14, local copies, waits for them, and re-layouts  10.7 us
    all_to_all x1, starting transfers between devices, local(): lax.all_to_all(picked, 'expert', split_axis=0, concat_axis=0, tiled=True)  6.35 us
    all_to_all x1, waiting for transfers between devices, local(): lax.all_to_all(picked, 'expert', split_axis=0, concat_axis=0, tiled=True)  6.04 us
    dot_general x2, matrix products, local(): jnp.dot(saved_rows.T, scaled_rows, preferred_element_type=jnp.float32)  5.47 us
    reduce_sum x1, other arithmetic, local(): update_sq = jnp.sum(update * update, axis=(1, 2))  3.4 us
  transfers between devices with their start and end apart: 3, of which 3 were waited for; matrix products, arithmetic and copies ran while one was open for 7% of the time, Pallas kernels for 0%

commit v1 on v0

--- a/solution.py
+++ b/solution.py
@@ -1,6 +1,10 @@
+import functools
+
 import jax
 import jax.numpy as jnp
 from jax import lax
+from jax.experimental import pallas as pl
+from jax.experimental.pallas import tpu as pltpu
 from jax.sharding import PartitionSpec as P
 
 learn_rate = 0.3
@@ -9,6 +13,392 @@
 norm_eps = 1e-06
 bias_one = 1.0 - 0.9**10
 bias_two = 1.0 - 0.999**10
+
+
+MESH = pl.DeviceIdType.MESH
+LANES = 128
+CHUNKS = 4
+
+
+def fused_kernel(
+    n_expert,
+    chunks,
+    token_ref,
+    count_ref,
+    mix_ref,
+    grad_hbm,
+    hidden_hbm,
+    weight_hbm,
+    first_hbm,
+    second_hbm,
+    out_hbm,
+    grad,
+    hidden,
+    weight,
+    first,
+    second,
+    outbuf,
+    sendbuf,
+    rows,
+    hsend,
+    hrecv,
+    lhs,
+    gradient,
+    update,
+    norms,
+    load_sem,
+    out_sem,
+    z_send,
+    z_recv,
+    p_send,
+    p_recv,
+    h_send,
+    h_recv,
+    n_send,
+    n_recv,
+):
+    e = lax.axis_index("expert")
+    d = lax.axis_index("dp")
+    core, x, y = d % 2, (d // 2) % 2, d // 4
+    experts_here, share, width = weight.shape
+    capacity = token_ref.shape[2]
+    cols = width // chunks
+    slots = experts_here * capacity
+    local_rows = n_expert * slots
+    pack = LANES // local_rows
+    n_dp = hrecv.shape[0]
+    half = n_expert // 2
+
+    def member(fy, fx, fc):
+        yy = 1 - y if fy else y
+        xx = 1 - x if fx else x
+        cc = 1 - core if fc else core
+        return yy * 4 + xx * 2 + cc
+
+    flips = [(f // 4, (f // 2) % 2, f % 2) for f in range(1, n_dp)]
+
+    barrier = pltpu.get_barrier_semaphore()
+    for step in range(1, n_expert):
+        pl.semaphore_signal(barrier, inc=1, device_id=((e + step) % n_expert, d), device_id_type=MESH)
+    for flip in flips:
+        pl.semaphore_signal(barrier, inc=1, device_id=(e, member(*flip)), device_id_type=MESH)
+
+    loads = [
+        pltpu.make_async_copy(src, dst, load_sem.at[i])
+        for i, (src, dst) in enumerate(
+            [
+                (grad_hbm, grad),
+                (hidden_hbm, hidden),
+                (weight_hbm, weight),
+                (first_hbm, first),
+                (second_hbm, second),
+            ]
+        )
+    ]
+    for copy in loads:
+        copy.start()
+
+    tokens = grad.shape[0]
+    lane = lax.broadcasted_iota(jnp.int32, (8, tokens), 1)
+    sub = lax.broadcasted_iota(jnp.int32, (8, tokens), 0)
+    blocks = []
+    for base in range(0, local_rows, 8):
+        want = jnp.zeros((8, tokens), jnp.int32)
+        for i in range(8):
+            s = base + i
+            want = jnp.where(sub == i, token_ref[0, s // capacity, s % capacity], want)
+        blocks.append(jnp.where(want == lane, 1.0, 0.0))
+    onehot = jnp.concatenate(blocks, axis=0).astype(jnp.bfloat16)
+    loads[0].wait()
+    for ch in range(chunks):
+        picked = jnp.dot(
+            onehot, grad[:, ch * cols : (ch + 1) * cols], preferred_element_type=jnp.float32
+        ).astype(jnp.bfloat16)
+        sendbuf[ch] = picked.reshape(n_expert, slots, cols)
+    for ch in range(chunks):
+        rows[ch, d, e] = sendbuf[ch, e]
+
+    pl.semaphore_wait(barrier, n_expert - 1 + n_dp - 1)
+
+    z_copies = []
+    for ch in range(chunks):
+        group = []
+        for step in range(1, n_expert):
+            peer = (e + step) % n_expert
+            copy = pltpu.make_async_remote_copy(
+                src_ref=sendbuf.at[ch, peer],
+                dst_ref=rows.at[ch, d, e],
+                send_sem=z_send.at[ch, step - 1],
+                recv_sem=z_recv.at[ch, step - 1],
+                device_id=(peer, d),
+                device_id_type=MESH,
+            )
+            copy.start()
+            group.append(copy)
+        z_copies.append(group)
+
+    slot = lax.broadcasted_iota(jnp.int32, (1, LANES), 1) % local_rows
+    live = jnp.zeros((1, LANES), jnp.int32)
+    for g in range(local_rows // capacity):
+        live = jnp.where(slot // capacity == g, count_ref[0, g], live)
+    mix = jnp.concatenate([mix_ref[...]] * pack, axis=1)
+    mix = jnp.where(slot % capacity < live, mix, 0.0).astype(jnp.bfloat16).astype(jnp.float32)
+    row_id = lax.broadcasted_iota(jnp.int32, (local_rows, LANES), 0)
+    col_id = lax.broadcasted_iota(jnp.int32, (local_rows, LANES), 1)
+    placed = jnp.where(col_id == row_id + (d % pack) * local_rows, mix, 0.0).astype(jnp.bfloat16)
+    loads[1].wait()
+    turned = lax.dot_general(
+        hidden[...], placed, (((0,), (0,)), ((), ())), preferred_element_type=jnp.float32
+    ).astype(jnp.bfloat16)
+    hsend[...] = turned.reshape(n_dp, share, LANES)
+    h_copies = []
+    for i, flip in enumerate(flips):
+        peer = member(*flip)
+        copy = pltpu.make_async_remote_copy(
+            src_ref=hsend.at[peer],
+            dst_ref=hrecv.at[d],
+            send_sem=h_send.at[i],
+            recv_sem=h_recv.at[i],
+            device_id=(e, peer),
+            device_id_type=MESH,
+        )
+        copy.start()
+        h_copies.append(copy)
+    hrecv[d] = hsend[d]
+
+    near_x, near_y, partner = member(0, 1, 0), member(1, 0, 0), member(0, 0, 1)
+    across = member(1, 1, 0)
+
+    def send(kind, ch, block, part, to):
+        ref = rows.at[ch, block] if part is None else rows.at[ch, block, pl.ds(*part)]
+        return pltpu.make_async_remote_copy(
+            src_ref=ref,
+            dst_ref=ref,
+            send_sem=p_send.at[ch, kind],
+            recv_sem=p_recv.at[ch, kind],
+            device_id=(e, to),
+            device_id_type=MESH,
+        )
+
+    low, high = (0, half), (half, n_expert - half)
+    plane = []
+    for ch in range(chunks):
+        plane.append(
+            dict(
+                own_x=send(0, ch, d, None, near_x),
+                own_y=send(1, ch, d, None, near_y),
+                own_c=send(2, ch, d, None, partner),
+                relay_y=send(3, ch, near_x, low, near_y),
+                relay_x=send(4, ch, near_y, high, near_x),
+                pass_x=send(5, ch, near_x, None, partner),
+                pass_y=send(6, ch, near_y, None, partner),
+                pass_low=send(7, ch, across, low, partner),
+                pass_high=send(8, ch, across, high, partner),
+            )
+        )
+
+    def stage_own(ch):
+        for copy in z_copies[ch]:
+            copy.wait_recv()
+        p = plane[ch]
+        for name in ("own_x", "own_y", "own_c"):
+            p[name].start()
+
+    def stage_relay(ch):
+        p = plane[ch]
+        p["own_x"].wait_recv()
+        p["relay_y"].start()
+        p["pass_x"].start()
+        p["own_y"].wait_recv()
+        p["relay_x"].start()
+        p["pass_y"].start()
+
+    def stage_pass(ch):
+        p = plane[ch]
+        p["relay_y"].wait_recv()
+        p["pass_low"].start()
+        p["relay_x"].wait_recv()
+        p["pass_high"].start()
+
+    def stage_lhs():
+        for copy in h_copies:
+            copy.wait_recv()
+        kind = (lax.broadcasted_iota(jnp.int32, (share, LANES), 1) % slots) // capacity
+        for q in range(n_dp // pack):
+            block = hrecv[q * pack].astype(jnp.float32)
+            for r in range(1, pack):
+                block = block + hrecv[q * pack + r].astype(jnp.float32)
+            for j in range(experts_here):
+                lhs[j * share : (j + 1) * share, q * LANES : (q + 1) * LANES] = jnp.where(
+                    kind == j, block, 0.0
+                ).astype(jnp.bfloat16)
+        for copy in loads[2:]:
+            copy.wait()
+
+    tile = 16
+    zero = jnp.zeros((tile, LANES), jnp.float32)
+
+    def fold(value):
+        total = value[:, :LANES]
+        for at in range(LANES, cols, LANES):
+            total = total + value[:, at : at + LANES]
+        return total
+
+    sums = [(zero, zero) for _ in range(experts_here)]
+
+    def stage_update(ch):
+        p = plane[ch]
+        for name in ("own_c", "pass_x", "pass_y", "pass_low", "pass_high"):
+            p[name].wait_recv()
+        gradient[...] = jnp.dot(
+            lhs[...], rows[ch].reshape(n_dp * local_rows, cols), preferred_element_type=jnp.float32
+        )
+        at = slice(ch * cols, (ch + 1) * cols)
+        for j in range(experts_here):
+
+            def block(r, carry, j=j):
+                here = pl.ds(pl.multiple_of(r * tile, tile), tile)
+                there = pl.ds(pl.multiple_of(j * share + r * tile, tile), tile)
+                g = gradient[there, :]
+                w = weight[j, here, at].astype(jnp.float32)
+                m = 0.9 * first[j, here, at].astype(jnp.float32) + 0.1 * g
+                v = 0.999 * second[j, here, at].astype(jnp.float32) + 0.001 * g * g
+                u = m / bias_one / (jnp.sqrt(v / bias_two) + adam_eps) + decay_rate * w
+                update[there, at] = u
+                return carry[0] + fold(w * w), carry[1] + fold(u * u)
+
+            sums[j] = lax.fori_loop(0, share // tile, block, sums[j])
+
+    for t in range(chunks + 3):
+        if t < chunks:
+            stage_own(t)
+        if 0 <= t - 1 < chunks:
+            stage_relay(t - 1)
+        if 0 <= t - 2 < chunks:
+            stage_pass(t - 2)
+        if t == 2:
+            stage_lhs()
+        if 0 <= t - 3 < chunks:
+            stage_update(t - 3)
+
+    for j in range(experts_here):
+        norms[d, j : j + 1, :] = jnp.sum(sums[j][0], axis=0, keepdims=True)
+        norms[d, experts_here + j : experts_here + j + 1, :] = jnp.sum(sums[j][1], axis=0, keepdims=True)
+    n_copies = []
+    for i, flip in enumerate(flips):
+        copy = pltpu.make_async_remote_copy(
+            src_ref=norms.at[d],
+            dst_ref=norms.at[d],
+            send_sem=n_send.at[i],
+            recv_sem=n_recv.at[i],
+            device_id=(e, member(*flip)),
+            device_id_type=MESH,
+        )
+        copy.start()
+        n_copies.append(copy)
+    for group in z_copies:
+        for copy in group:
+            copy.wait_send()
+    for p in plane:
+        for copy in p.values():
+            copy.wait_send()
+    for copy in h_copies:
+        copy.wait_send()
+    for copy in n_copies:
+        copy.wait_recv()
+    total = norms[0]
+    for i in range(1, n_dp):
+        total = total + norms[i]
+    total = jnp.sqrt(jnp.sum(total, axis=1, keepdims=True))
+    outs = []
+    for j in range(experts_here):
+        ratio = total[j : j + 1] / (total[experts_here + j : experts_here + j + 1] + norm_eps)
+        scale = learn_rate * ratio
+
+        def finish(r, carry, j=j, scale=scale):
+            here = pl.ds(pl.multiple_of(r * tile, tile), tile)
+            there = pl.ds(pl.multiple_of(j * share + r * tile, tile), tile)
+            fresh = weight[j, here, :].astype(jnp.float32) - scale * update[there, :]
+            outbuf[j, here, :] = fresh.astype(jnp.bfloat16)
+            return carry
+
+        lax.fori_loop(0, share // tile, finish, 0)
+        copy = pltpu.make_async_copy(outbuf.at[j], out_hbm.at[j], out_sem.at[j])
+        copy.start()
+        outs.append(copy)
+    for copy in n_copies:
+        copy.wait_send()
+    for copy in outs:
+        copy.wait()
+
+
+def fused(n_expert, n_dp, grad_out, slot_token, hidden, slot_weight, counts, master_weight, moment1, moment2):
+    experts_here, share, width = master_weight.shape
+    capacity = slot_token.shape[2]
+    slots = experts_here * capacity
+    local_rows = n_expert * slots
+    cols = width // CHUNKS
+    half_type = jnp.bfloat16
+    dma = pltpu.SemaphoreType.DMA
+    anywhere = pl.BlockSpec(memory_space=pl.ANY)
+    return pl.pallas_call(
+        functools.partial(fused_kernel, n_expert, CHUNKS),
+        out_shape=jax.ShapeDtypeStruct(master_weight.shape, half_type),
+        in_specs=[
+            pl.BlockSpec(memory_space=pltpu.SMEM),
+            pl.BlockSpec(memory_space=pltpu.SMEM),
+            pl.BlockSpec(memory_space=pltpu.VMEM),
+        ]
+        + [anywhere] * 5,
+        out_specs=anywhere,
+        scratch_shapes=[
+            pltpu.VMEM(grad_out.shape, half_type),
+            pltpu.VMEM(hidden.shape, half_type),
+            pltpu.VMEM(master_weight.shape, half_type),
+            pltpu.VMEM(master_weight.shape, half_type),
+            pltpu.VMEM(master_weight.shape, half_type),
+            pltpu.VMEM(master_weight.shape, half_type),
+            pltpu.VMEM((CHUNKS, n_expert, slots, cols), half_type),
+            pltpu.VMEM((CHUNKS, n_dp, n_expert, slots, cols), half_type),
+            pltpu.VMEM((n_dp, share, LANES), half_type),
+            pltpu.VMEM((n_dp, share, LANES), half_type),
+            pltpu.VMEM((experts_here * share, n_dp * local_rows), half_type),
+            pltpu.VMEM((experts_here * share, cols), jnp.float32),
+            pltpu.VMEM((experts_here * share, width), jnp.float32),
+            pltpu.VMEM((n_dp, 2 * experts_here, LANES), jnp.float32),
+            dma((5,)),
+            dma((experts_here,)),
+            dma((CHUNKS, n_expert - 1)),
+            dma((CHUNKS, n_expert - 1)),
+            dma((CHUNKS, 9)),
+            dma((CHUNKS, 9)),
+            dma((n_dp - 1,)),
+            dma((n_dp - 1,)),
+            dma((n_dp - 1,)),
+            dma((n_dp - 1,)),
+        ],
+        compiler_params=pltpu.CompilerParams(collective_id=0, has_side_effects=True),
+    )(slot_token, counts, slot_weight, grad_out, hidden, master_weight, moment1, moment2)
+
+
+def choose(n_expert, n_dp, *args):
+    grad_out, slot_token, hidden, _, _, master_weight, _, _ = args
+    experts_here, share, width = master_weight.shape
+    capacity = slot_token.shape[2]
+    local_rows = hidden.shape[0]
+    fewer_rows = n_dp * n_expert * capacity < hidden.shape[1]
+    cube = n_dp == 2**3 and n_expert % 2 == 0
+    tiles = (
+        LANES % local_rows == 0
+        and local_rows % 8 == 0
+        and n_dp % max(1, LANES // local_rows) == 0
+        and (experts_here * capacity) % 16 == 0
+        and share % 16 == 0
+        and width % (CHUNKS * LANES) == 0
+    )
+    if fewer_rows and cube and tiles:
+        return fused(n_expert, n_dp, *args)
+    return local(*args)
 
 
 def local(grad_out, slot_token, hidden, slot_weight, counts, master_weight, moment1, moment2):
@@ -73,6 +463,7 @@
         P("expert", "dp", None),
         P("expert", "dp", None),
     )
+    step = functools.partial(choose, mesh.shape["expert"], mesh.shape["dp"])
     return jax.shard_map(
-        local, mesh=mesh, in_specs=placed, out_specs=P("expert", "dp", None), check_vma=False
-    )
+        step, mesh=mesh, in_specs=placed, out_specs=P("expert", "dp", None), check_vma=False
+    )

time: 152 us -> 33.1 us (0.22)
  waiting for transfers between devices: 93.3 us -> 0 us
  Pallas kernels: 0 us -> 30.8 us
  between operations: 13.5 us -> 0.01 us
  blocking collectives: 12.5 us -> 0 us
  local copies, waits for them, and re-layouts: 13.2 us -> 2.09 us
  other arithmetic: 6.99 us -> 0 us
  starting transfers between devices: 6.39 us -> 0 us
  matrix products: 5.47 us -> 0 us
    reduce_scatter x2 -> x0, waiting for transfers between devices: 87.2 us -> none  [local(): lax.psum_scatter(term.astype(jnp.bfloat16).astype(jnp.float32).astype(jnp...]
    pallas_call x0 -> x1, Pallas kernels: none -> 30.8 us  [fused(): pl.pallas_call(functools.partial(fused_kernel, n_expert, CHUNKS), out_sha...]
    psum x1 -> x0, blocking collectives: 12.5 us -> none  [local(): update_total = lax.psum(update_sq, 'dp')]
    unnamed x14 -> x1, local copies, waits for them, and re-layouts: 10.7 us -> 2.09 us
    all_to_all x1 -> x0, starting transfers between devices: 6.35 us -> none  [local(): lax.all_to_all(picked, 'expert', split_axis=0, concat_axis=0, tiled=True)]
    all_to_all x1 -> x0, waiting for transfers between devices: 6.04 us -> none  [local(): lax.all_to_all(picked, 'expert', split_axis=0, concat_axis=0, tiled=True)]
    dot_general x2 -> x0, matrix products: 5.47 us -> none  [local(): jnp.dot(saved_rows.T, scaled_rows, preferred_element_type=jnp.float32)]
    reduce_sum x1 -> x0, other arithmetic: 3.4 us -> none  [local(): update_sq = jnp.sum(update * update, axis=(1, 2))]
  transfers between devices with their start and end apart: 3 -> 0, of which waited for: 3 -> 0; matrix products, arithmetic and copies ran while one was open for 7% -> 0% of each run, Pallas kernels for 0% -> 0%
where the time goes in v1:
time: 33.1 us; the launch traced here: 32.9 us
  Pallas kernels  30.8 us (93%)
  local copies, waits for them, and re-layouts  2.09 us (6%)
    pallas_call x1, Pallas kernels, fused(): pl.pallas_call(functools.partial(fused_kernel, n_expert, CHUNKS), out_sha...  30.8 us
    unnamed x1, local copies, waits for them, and re-layouts  2.09 us

profile of v1, /device:TPU:0, one launch (start us, length us, event | category | flops | bytes accessed | tf_op | source)
XLA Modules:
  0.0 32.9 jit_solution(14703111092055934825)
XLA Ops:
  0.0 30.8 %shard_map.82 = bf16[2,96,2048]{2,1,0:T(8,128)(2,1)} custom-call(s32[1,8,8]{2,1,0:T(8,128)} %token_ref.1, s32[1,8]{1,0:T(1,128)} %count_ref.1, f32[1,64]{1,0:T(1,128)} %mix_ref.1, bf16[128,2048]{1,0:T(8,128)(2,1)} %grad_hbm.1, bf16[64,768]{1,0:T(8,128)(2,1)} %hidden_hbm.1, bf16[2,96,2048]{2,1,0:T(8,128)(2,1)} %weight_hbm.1, bf16[2,96,2048]{2,1,0:T(8,128)(2,1)} %first_hbm.1, ...), custom_call_target="tpu_custom_call" | custom-call | tf_op jit(solution)/shard_map/pallas_call | solution.py:344
  30.8 2.1 %copy.10 = bf16[2,96,2048]{2,1,0:T(8,128)(2,1)} copy(bf16[2,96,2048]{2,1,0:T(8,128)(2,1)} %shard_map.82) | data formatting | bytes 1572864

commit v2 on v1

--- a/solution.py
+++ b/solution.py
@@ -17,7 +17,19 @@
 
 MESH = pl.DeviceIdType.MESH
 LANES = 128
-CHUNKS = 4
+CHUNKS = 2
+
+
+def mix_column(mix_ref, count_ref, local_rows, capacity):
+    row = lax.broadcasted_iota(jnp.int32, (local_rows, local_rows), 0)
+    col = lax.broadcasted_iota(jnp.int32, (local_rows, local_rows), 1)
+    lane = lax.broadcasted_iota(jnp.int32, (1, local_rows), 1)
+    live = jnp.zeros((1, local_rows), jnp.int32)
+    for g in range(local_rows // capacity):
+        live = jnp.where(lane // capacity == g, count_ref[0, g], live)
+    mix = jnp.where(lane % capacity < live, mix_ref[...], 0.0)
+    mix = mix.astype(jnp.bfloat16).astype(jnp.float32)
+    return jnp.sum(jnp.where(row == col, mix, 0.0), axis=1, keepdims=True)
 
 
 def fused_kernel(
@@ -32,12 +44,12 @@
     first_hbm,
     second_hbm,
     out_hbm,
+    scale_ref,
     grad,
     hidden,
     weight,
     first,
     second,
-    outbuf,
     sendbuf,
     rows,
     hsend,
@@ -65,9 +77,9 @@
     cols = width // chunks
     slots = experts_here * capacity
     local_rows = n_expert * slots
-    pack = LANES // local_rows
     n_dp = hrecv.shape[0]
-    half = n_expert // 2
+    folds = LANES // local_rows
+    part = share // folds
 
     def member(fy, fx, fc):
         yy = 1 - y if fy else y
@@ -87,16 +99,33 @@
         pltpu.make_async_copy(src, dst, load_sem.at[i])
         for i, (src, dst) in enumerate(
             [
+                (hidden_hbm, hidden),
                 (grad_hbm, grad),
-                (hidden_hbm, hidden),
                 (weight_hbm, weight),
                 (first_hbm, first),
                 (second_hbm, second),
             ]
         )
     ]
-    for copy in loads:
-        copy.start()
+    loads[0].start()
+    loads[1].start()
+
+    slot = lax.broadcasted_iota(jnp.int32, (1, LANES), 1) % local_rows
+    source = (slot // slots + e) % n_expert * slots + slot % slots
+    row_id = lax.broadcasted_iota(jnp.int32, (local_rows, LANES), 0)
+    mix_rows = mix_column(mix_ref, count_ref, local_rows, capacity)
+    placed = jnp.where(row_id == source, mix_rows, 0.0).astype(jnp.bfloat16)
+    loads[0].wait()
+    turned = lax.dot_general(
+        hidden[...], placed, (((0,), (0,)), ((), ())), preferred_element_type=jnp.float32
+    )
+    turned = turned.reshape(n_dp, folds, part, LANES)
+    at_lane = lax.broadcasted_iota(jnp.int32, (1, 1, LANES), 2) // local_rows
+    dense = turned[:, 0]
+    for f in range(1, folds):
+        dense = jnp.where(at_lane == f, turned[:, f], dense)
+    hsend[...] = dense.astype(jnp.bfloat16)
+    hrecv[d] = hsend[d]
 
     tokens = grad.shape[0]
     lane = lax.broadcasted_iota(jnp.int32, (8, tokens), 1)
@@ -109,14 +138,16 @@
             want = jnp.where(sub == i, token_ref[0, s // capacity, s % capacity], want)
         blocks.append(jnp.where(want == lane, 1.0, 0.0))
     onehot = jnp.concatenate(blocks, axis=0).astype(jnp.bfloat16)
-    loads[0].wait()
+    loads[1].wait()
+    for copy in loads[2:]:
+        copy.start()
     for ch in range(chunks):
         picked = jnp.dot(
             onehot, grad[:, ch * cols : (ch + 1) * cols], preferred_element_type=jnp.float32
         ).astype(jnp.bfloat16)
         sendbuf[ch] = picked.reshape(n_expert, slots, cols)
     for ch in range(chunks):
-        rows[ch, d, e] = sendbuf[ch, e]
+        rows[ch, d, 0] = sendbuf[ch, e]
 
     pl.semaphore_wait(barrier, n_expert - 1 + n_dp - 1)
 
@@ -127,7 +158,7 @@
             peer = (e + step) % n_expert
             copy = pltpu.make_async_remote_copy(
                 src_ref=sendbuf.at[ch, peer],
-                dst_ref=rows.at[ch, d, e],
+                dst_ref=rows.at[ch, d, n_expert - step],
                 send_sem=z_send.at[ch, step - 1],
                 recv_sem=z_recv.at[ch, step - 1],
                 device_id=(peer, d),
@@ -137,20 +168,46 @@
             group.append(copy)
         z_copies.append(group)
 
-    slot = lax.broadcasted_iota(jnp.int32, (1, LANES), 1) % local_rows
-    live = jnp.zeros((1, LANES), jnp.int32)
-    for g in range(local_rows // capacity):
-        live = jnp.where(slot // capacity == g, count_ref[0, g], live)
-    mix = jnp.concatenate([mix_ref[...]] * pack, axis=1)
-    mix = jnp.where(slot % capacity < live, mix, 0.0).astype(jnp.bfloat16).astype(jnp.float32)
-    row_id = lax.broadcasted_iota(jnp.int32, (local_rows, LANES), 0)
-    col_id = lax.broadcasted_iota(jnp.int32, (local_rows, LANES), 1)
-    placed = jnp.where(col_id == row_id + (d % pack) * local_rows, mix, 0.0).astype(jnp.bfloat16)
-    loads[1].wait()
-    turned = lax.dot_general(
-        hidden[...], placed, (((0,), (0,)), ((), ())), preferred_element_type=jnp.float32
-    ).astype(jnp.bfloat16)
-    hsend[...] = turned.reshape(n_dp, share, LANES)
+    near_x, near_y, partner = member(0, 1, 0), member(1, 0, 0), member(0, 0, 1)
+    across = member(1, 1, 0)
+
+    def region(piece, block, which):
+        if piece == 0:
+            start, size = [(0, chunks), (0, chunks // 2), (chunks // 2, chunks - chunks // 2)][which]
+            return rows.at[pl.ds(start, size), block, 0]
+        others = n_expert - 1
+        low = others // 2 if piece % 2 else others - others // 2
+        start, size = [(1, others), (1, low), (1 + low, others - low)][which]
+        return rows.at[piece - 1, block, pl.ds(start, size)]
+
+    def send(kind, piece, block, which, to):
+        ref = region(piece, block, which)
+        return pltpu.make_async_remote_copy(
+            src_ref=ref,
+            dst_ref=ref,
+            send_sem=p_send.at[piece, kind],
+            recv_sem=p_recv.at[piece, kind],
+            device_id=(e, to),
+            device_id_type=MESH,
+        )
+
+    whole, low, high = 0, 1, 2
+    plane = []
+    for piece in range(chunks + 1):
+        plane.append(
+            dict(
+                own_x=send(0, piece, d, whole, near_x),
+                own_y=send(1, piece, d, whole, near_y),
+                own_c=send(2, piece, d, whole, partner),
+                relay_y=send(3, piece, near_x, low, near_y),
+                relay_x=send(4, piece, near_y, high, near_x),
+                pass_x=send(5, piece, near_x, whole, partner),
+                pass_y=send(6, piece, near_y, whole, partner),
+                pass_low=send(7, piece, across, low, partner),
+                pass_high=send(8, piece, across, high, partner),
+            )
+        )
+
     h_copies = []
     for i, flip in enumerate(flips):
         peer = member(*flip)
@@ -162,47 +219,18 @@
             device_id=(e, peer),
             device_id_type=MESH,
         )
-        copy.start()
         h_copies.append(copy)
-    hrecv[d] = hsend[d]
-
-    near_x, near_y, partner = member(0, 1, 0), member(1, 0, 0), member(0, 0, 1)
-    across = member(1, 1, 0)
-
-    def send(kind, ch, block, part, to):
-        ref = rows.at[ch, block] if part is None else rows.at[ch, block, pl.ds(*part)]
-        return pltpu.make_async_remote_copy(
-            src_ref=ref,
-            dst_ref=ref,
-            send_sem=p_send.at[ch, kind],
-            recv_sem=p_recv.at[ch, kind],
-            device_id=(e, to),
-            device_id_type=MESH,
-        )
-
-    low, high = (0, half), (half, n_expert - half)
-    plane = []
-    for ch in range(chunks):
-        plane.append(
-            dict(
-                own_x=send(0, ch, d, None, near_x),
-                own_y=send(1, ch, d, None, near_y),
-                own_c=send(2, ch, d, None, partner),
-                relay_y=send(3, ch, near_x, low, near_y),
-                relay_x=send(4, ch, near_y, high, near_x),
-                pass_x=send(5, ch, near_x, None, partner),
-                pass_y=send(6, ch, near_y, None, partner),
-                pass_low=send(7, ch, across, low, partner),
-                pass_high=send(8, ch, across, high, partner),
-            )
-        )
 
     def stage_own(ch):
-        for copy in z_copies[ch]:
-            copy.wait_recv()
+        if ch > 0:
+            for copy in z_copies[ch - 1]:
+                copy.wait_recv()
         p = plane[ch]
         for name in ("own_x", "own_y", "own_c"):
             p[name].start()
+        if ch == 0:
+            for copy in h_copies:
+                copy.start()
 
     def stage_relay(ch):
         p = plane[ch]
@@ -223,15 +251,21 @@
     def stage_lhs():
         for copy in h_copies:
             copy.wait_recv()
-        kind = (lax.broadcasted_iota(jnp.int32, (share, LANES), 1) % slots) // capacity
-        for q in range(n_dp // pack):
-            block = hrecv[q * pack].astype(jnp.float32)
-            for r in range(1, pack):
-                block = block + hrecv[q * pack + r].astype(jnp.float32)
-            for j in range(experts_here):
-                lhs[j * share : (j + 1) * share, q * LANES : (q + 1) * LANES] = jnp.where(
-                    kind == j, block, 0.0
-                ).astype(jnp.bfloat16)
+        lane_part = lax.broadcasted_iota(jnp.int32, (part, LANES), 1) // local_rows
+        kind = (lax.broadcasted_iota(jnp.int32, (part, LANES), 1) % slots) // capacity
+        for q in range(n_dp // folds):
+            for f in range(folds):
+                block = jnp.zeros((part, LANES), jnp.float32)
+                for r in range(folds):
+                    piece = hrecv[q * folds + r].astype(jnp.float32)
+                    if r != f:
+                        piece = pltpu.roll(piece, (r - f) % folds * local_rows, 1)
+                    block = jnp.where(lane_part == r, piece, block)
+                for j in range(experts_here):
+                    top = j * share + f * part
+                    lhs[top : top + part, q * LANES : (q + 1) * LANES] = jnp.where(
+                        kind == j, block, 0.0
+                    ).astype(jnp.bfloat16)
         for copy in loads[2:]:
             copy.wait()
 
@@ -245,11 +279,16 @@
         return total
 
     sums = [(zero, zero) for _ in range(experts_here)]
-
-    def stage_update(ch):
-        p = plane[ch]
+    outs = []
+
+    def stage_update(piece):
+        p = plane[piece]
         for name in ("own_c", "pass_x", "pass_y", "pass_low", "pass_high"):
             p[name].wait_recv()
+        if piece == 0:
+            stage_lhs()
+            return
+        ch = piece - 1
         gradient[...] = jnp.dot(
             lhs[...], rows[ch].reshape(n_dp * local_rows, cols), preferred_element_type=jnp.float32
         )
@@ -264,21 +303,23 @@
                 m = 0.9 * first[j, here, at].astype(jnp.float32) + 0.1 * g
                 v = 0.999 * second[j, here, at].astype(jnp.float32) + 0.001 * g * g
                 u = m / bias_one / (jnp.sqrt(v / bias_two) + adam_eps) + decay_rate * w
-                update[there, at] = u
+                update[there, at] = u.astype(jnp.bfloat16)
                 return carry[0] + fold(w * w), carry[1] + fold(u * u)
 
             sums[j] = lax.fori_loop(0, share // tile, block, sums[j])
-
-    for t in range(chunks + 3):
-        if t < chunks:
+        copy = pltpu.make_async_copy(update.at[:, at], out_hbm.at[:, at], out_sem.at[ch])
+        copy.start()
+        outs.append(copy)
+
+    pieces = chunks + 1
+    for t in range(pieces + 3):
+        if t < pieces:
             stage_own(t)
-        if 0 <= t - 1 < chunks:
+        if 0 <= t - 1 < pieces:
             stage_relay(t - 1)
-        if 0 <= t - 2 < chunks:
+        if 0 <= t - 2 < pieces:
             stage_pass(t - 2)
-        if t == 2:
-            stage_lhs()
-        if 0 <= t - 3 < chunks:
+        if 0 <= t - 3 < pieces:
             stage_update(t - 3)
 
     for j in range(experts_here):
@@ -310,22 +351,9 @@
     for i in range(1, n_dp):
         total = total + norms[i]
     total = jnp.sqrt(jnp.sum(total, axis=1, keepdims=True))
-    outs = []
     for j in range(experts_here):
         ratio = total[j : j + 1] / (total[experts_here + j : experts_here + j + 1] + norm_eps)
-        scale = learn_rate * ratio
-
-        def finish(r, carry, j=j, scale=scale):
-            here = pl.ds(pl.multiple_of(r * tile, tile), tile)
-            there = pl.ds(pl.multiple_of(j * share + r * tile, tile), tile)
-            fresh = weight[j, here, :].astype(jnp.float32) - scale * update[there, :]
-            outbuf[j, here, :] = fresh.astype(jnp.bfloat16)
-            return carry
-
-        lax.fori_loop(0, share // tile, finish, 0)
-        copy = pltpu.make_async_copy(outbuf.at[j], out_hbm.at[j], out_sem.at[j])
-        copy.start()
-        outs.append(copy)
+        scale_ref[j : j + 1, :] = jnp.broadcast_to(learn_rate * ratio, (1, width))
     for copy in n_copies:
         copy.wait_send()
     for copy in outs:
@@ -341,37 +369,39 @@
     half_type = jnp.bfloat16
     dma = pltpu.SemaphoreType.DMA
     anywhere = pl.BlockSpec(memory_space=pl.ANY)
-    return pl.pallas_call(
+    update, scale = pl.pallas_call(
         functools.partial(fused_kernel, n_expert, CHUNKS),
-        out_shape=jax.ShapeDtypeStruct(master_weight.shape, half_type),
+        out_shape=(
+            jax.ShapeDtypeStruct((experts_here * share, width), half_type),
+            jax.ShapeDtypeStruct((experts_here, width), jnp.float32),
+        ),
         in_specs=[
             pl.BlockSpec(memory_space=pltpu.SMEM),
             pl.BlockSpec(memory_space=pltpu.SMEM),
             pl.BlockSpec(memory_space=pltpu.VMEM),
         ]
         + [anywhere] * 5,
-        out_specs=anywhere,
+        out_specs=(anywhere, pl.BlockSpec(memory_space=pltpu.VMEM)),
         scratch_shapes=[
             pltpu.VMEM(grad_out.shape, half_type),
             pltpu.VMEM(hidden.shape, half_type),
             pltpu.VMEM(master_weight.shape, half_type),
             pltpu.VMEM(master_weight.shape, half_type),
             pltpu.VMEM(master_weight.shape, half_type),
-            pltpu.VMEM(master_weight.shape, half_type),
             pltpu.VMEM((CHUNKS, n_expert, slots, cols), half_type),
             pltpu.VMEM((CHUNKS, n_dp, n_expert, slots, cols), half_type),
-            pltpu.VMEM((n_dp, share, LANES), half_type),
-            pltpu.VMEM((n_dp, share, LANES), half_type),
+            pltpu.VMEM((n_dp, share * local_rows // LANES, LANES), half_type),
+            pltpu.VMEM((n_dp, share * local_rows // LANES, LANES), half_type),
             pltpu.VMEM((experts_here * share, n_dp * local_rows), half_type),
             pltpu.VMEM((experts_here * share, cols), jnp.float32),
-            pltpu.VMEM((experts_here * share, width), jnp.float32),
+            pltpu.VMEM((experts_here * share, width), half_type),
             pltpu.VMEM((n_dp, 2 * experts_here, LANES), jnp.float32),
             dma((5,)),
-            dma((experts_here,)),
+            dma((CHUNKS,)),
             dma((CHUNKS, n_expert - 1)),
             dma((CHUNKS, n_expert - 1)),
-            dma((CHUNKS, 9)),
-            dma((CHUNKS, 9)),
+            dma((CHUNKS + 1, 9)),
+            dma((CHUNKS + 1, 9)),
             dma((n_dp - 1,)),
             dma((n_dp - 1,)),
             dma((n_dp - 1,)),
@@ -379,6 +409,9 @@
         ],
         compiler_params=pltpu.CompilerParams(collective_id=0, has_side_effects=True),
     )(slot_token, counts, slot_weight, grad_out, hidden, master_weight, moment1, moment2)
+    update = update.reshape(master_weight.shape).astype(jnp.float32)
+    fresh = master_weight.astype(jnp.float32) - scale[:, None, :] * update
+    return fresh.astype(master_weight.dtype)
 
 
 def choose(n_expert, n_dp, *args):
@@ -393,7 +426,7 @@
         and local_rows % 8 == 0
         and n_dp % max(1, LANES // local_rows) == 0
         and (experts_here * capacity) % 16 == 0
-        and share % 16 == 0
+        and share % (16 * max(1, LANES // local_rows)) == 0
         and width % (CHUNKS * LANES) == 0
     )
     if fewer_rows and cube and tiles:

time: 33.1 us -> 31 us (0.937)
  Pallas kernels: 30.8 us -> 28.5 us
  other arithmetic: 0 us -> 2.3 us
  local copies, waits for them, and re-layouts: 2.09 us -> 0.01 us
    pallas_call x1, Pallas kernels: 30.8 us -> 28.5 us  [fused(): pl.pallas_call(functools.partial(fused_kernel, n_expert, CHUNKS), out_sha...]
    convert_element_type x0 -> x1, other arithmetic: none -> 2.3 us  [fused(): return fresh.astype(master_weight.dtype)]
    unnamed x1 -> x2, local copies, waits for them, and re-layouts: 2.09 us -> 0.01 us
where the time goes in v2:
time: 31 us; the launch traced here: 30.8 us
  Pallas kernels  28.5 us (92%)
  other arithmetic  2.3 us (7%)
    pallas_call x1, Pallas kernels, fused(): pl.pallas_call(functools.partial(fused_kernel, n_expert, CHUNKS), out_sha...  28.5 us
    convert_element_type x1, other arithmetic, fused(): return fresh.astype(master_weight.dtype)  2.3 us

profile of v2, /device:TPU:0, one launch (start us, length us, event | category | flops | bytes accessed | tf_op | source)
XLA Modules:
  0.0 30.8 jit_solution(8636043526146585957)
XLA Ops:
  0.0 0.0 copy-start
  0.0 28.5 %shard_map.82 = (bf16[192,2048]{1,0:T(8,128)(2,1)}, f32[2,2048]{1,0:T(2,128)}) custom-call(s32[1,8,8]{2,1,0:T(8,128)} %token_ref.1, s32[1,8]{1,0:T(1,128)} %count_ref.1, f32[1,64]{1,0:T(1,128)} %mix_ref.1, bf16[128,2048]{1,0:T(8,128)(2,1)} %grad_hbm.1, bf16[64,768]{1,0:T(8,128)(2,1)} %hidden_hbm.1, bf16[2,96,2048]{2,1,0:T(8,128)(2,1)} %weight_hbm.1, ...), custom_call_target="tpu_custom_call" | custom-call | tf_op jit(solution)/shard_map/pallas_call | solution.py:372
  28.5 0.0 copy-done
  28.5 2.3 %fusion.1 = bf16[2,96,2048]{2,1,0:T(8,128)(2,1)} fusion(bf16[2,96,2048]{2,1,0:T(8,128)(2,1)} %bitcast.2, bf16[2,96,2048]{2,1,0:T(8,128)(2,1)S(1)} %copy-done, f32[2,2048]{1,0:T(2,128)} %get-tuple-element.7), kind=kLoop, calls=%fused_computation.2 | loop fusion | flops 1966080 | bytes 2375680 | tf_op jit(solution)/shard_map/convert_element_type | solution.py:414
Async XLA Ops:
  0.0 28.5 %copy-start = (bf16[2,96,2048]{2,1,0:T(8,128)(2,1)S(1)}, bf16[2,96,2048]{2,1,0:T(8,128)(2,1)}, u32[]{:S(2)}) copy-start(bf16[2,96,2048]{2,1,0:T(8,128)(2,1)} %weight_hbm.1) | copy-start | bytes 2359300

commit v3 on v2

--- a/solution.py
+++ b/solution.py
@@ -56,6 +56,9 @@
     hrecv,
     lhs,
     gradient,
+    known_w,
+    known_m,
+    known_v,
     update,
     norms,
     load_sem,
@@ -107,25 +110,8 @@
             ]
         )
     ]
+    loads[1].start()
     loads[0].start()
-    loads[1].start()
-
-    slot = lax.broadcasted_iota(jnp.int32, (1, LANES), 1) % local_rows
-    source = (slot // slots + e) % n_expert * slots + slot % slots
-    row_id = lax.broadcasted_iota(jnp.int32, (local_rows, LANES), 0)
-    mix_rows = mix_column(mix_ref, count_ref, local_rows, capacity)
-    placed = jnp.where(row_id == source, mix_rows, 0.0).astype(jnp.bfloat16)
-    loads[0].wait()
-    turned = lax.dot_general(
-        hidden[...], placed, (((0,), (0,)), ((), ())), preferred_element_type=jnp.float32
-    )
-    turned = turned.reshape(n_dp, folds, part, LANES)
-    at_lane = lax.broadcasted_iota(jnp.int32, (1, 1, LANES), 2) // local_rows
-    dense = turned[:, 0]
-    for f in range(1, folds):
-        dense = jnp.where(at_lane == f, turned[:, f], dense)
-    hsend[...] = dense.astype(jnp.bfloat16)
-    hrecv[d] = hsend[d]
 
     tokens = grad.shape[0]
     lane = lax.broadcasted_iota(jnp.int32, (8, tokens), 1)
@@ -141,18 +127,15 @@
     loads[1].wait()
     for copy in loads[2:]:
         copy.start()
+    z_copies = []
     for ch in range(chunks):
         picked = jnp.dot(
             onehot, grad[:, ch * cols : (ch + 1) * cols], preferred_element_type=jnp.float32
         ).astype(jnp.bfloat16)
         sendbuf[ch] = picked.reshape(n_expert, slots, cols)
-    for ch in range(chunks):
         rows[ch, d, 0] = sendbuf[ch, e]
-
-    pl.semaphore_wait(barrier, n_expert - 1 + n_dp - 1)
-
-    z_copies = []
-    for ch in range(chunks):
+        if ch == 0:
+            pl.semaphore_wait(barrier, n_expert - 1 + n_dp - 1)
         group = []
         for step in range(1, n_expert):
             peer = (e + step) % n_expert
@@ -221,6 +204,26 @@
         )
         h_copies.append(copy)
 
+    def stage_hidden():
+        slot = lax.broadcasted_iota(jnp.int32, (1, LANES), 1) % local_rows
+        source = (slot // slots + e) % n_expert * slots + slot % slots
+        row_id = lax.broadcasted_iota(jnp.int32, (local_rows, LANES), 0)
+        mix_rows = mix_column(mix_ref, count_ref, local_rows, capacity)
+        placed = jnp.where(row_id == source, mix_rows, 0.0).astype(jnp.bfloat16)
+        loads[0].wait()
+        turned = lax.dot_general(
+            hidden[...], placed, (((0,), (0,)), ((), ())), preferred_element_type=jnp.float32
+        )
+        turned = turned.reshape(n_dp, folds, part, LANES)
+        at_lane = lax.broadcasted_iota(jnp.int32, (1, 1, LANES), 2) // local_rows
+        dense = turned[:, 0]
+        for f in range(1, folds):
+            dense = jnp.where(at_lane == f, turned[:, f], dense)
+        hsend[...] = dense.astype(jnp.bfloat16)
+        hrecv[d] = hsend[d]
+        for copy in h_copies:
+            copy.start()
+
     def stage_own(ch):
         if ch > 0:
             for copy in z_copies[ch - 1]:
@@ -229,8 +232,9 @@
         for name in ("own_x", "own_y", "own_c"):
             p[name].start()
         if ch == 0:
-            for copy in h_copies:
-                copy.start()
+            stage_hidden()
+        if ch == 1:
+            stage_known()
 
     def stage_relay(ch):
         p = plane[ch]
@@ -266,19 +270,39 @@
                     lhs[top : top + part, q * LANES : (q + 1) * LANES] = jnp.where(
                         kind == j, block, 0.0
                     ).astype(jnp.bfloat16)
+
+    tile = 16
+    known_cols = cols
+    zero = jnp.zeros((tile, LANES), jnp.float32)
+
+    def fold(value):
+        total = value[:, :LANES]
+        for at in range(LANES, value.shape[1], LANES):
+            total = total + value[:, at : at + LANES]
+        return total
+
+    weight_sums = [zero for _ in range(experts_here)]
+    sums = [zero for _ in range(experts_here)]
+
+    def stage_known():
         for copy in loads[2:]:
             copy.wait()
-
-    tile = 16
-    zero = jnp.zeros((tile, LANES), jnp.float32)
-
-    def fold(value):
-        total = value[:, :LANES]
-        for at in range(LANES, cols, LANES):
-            total = total + value[:, at : at + LANES]
-        return total
-
-    sums = [(zero, zero) for _ in range(experts_here)]
+        for j in range(experts_here):
+
+            def block(r, carry, j=j):
+                here = pl.ds(pl.multiple_of(r * tile, tile), tile)
+                there = pl.ds(pl.multiple_of(j * share + r * tile, tile), tile)
+                for at in range(0, width, known_cols):
+                    part_at = slice(at, at + known_cols)
+                    w = weight[j, here, part_at].astype(jnp.float32)
+                    known_w[there, part_at] = decay_rate * w
+                    known_m[there, part_at] = (0.9 / bias_one) * first[j, here, part_at].astype(jnp.float32)
+                    known_v[there, part_at] = (0.999 / bias_two) * second[j, here, part_at].astype(jnp.float32)
+                    carry = carry + fold(w * w)
+                return carry
+
+            weight_sums[j] = lax.fori_loop(0, share // tile, block, weight_sums[j])
+
     outs = []
 
     def stage_update(piece):
@@ -296,15 +320,13 @@
         for j in range(experts_here):
 
             def block(r, carry, j=j):
-                here = pl.ds(pl.multiple_of(r * tile, tile), tile)
                 there = pl.ds(pl.multiple_of(j * share + r * tile, tile), tile)
                 g = gradient[there, :]
-                w = weight[j, here, at].astype(jnp.float32)
-                m = 0.9 * first[j, here, at].astype(jnp.float32) + 0.1 * g
-                v = 0.999 * second[j, here, at].astype(jnp.float32) + 0.001 * g * g
-                u = m / bias_one / (jnp.sqrt(v / bias_two) + adam_eps) + decay_rate * w
+                m = known_m[there, at] + (0.1 / bias_one) * g
+                v = known_v[there, at] + (0.001 / bias_two) * g * g
+                u = m / (v * lax.rsqrt(v) + adam_eps) + known_w[there, at]
                 update[there, at] = u.astype(jnp.bfloat16)
-                return carry[0] + fold(w * w), carry[1] + fold(u * u)
+                return carry + fold(u * u)
 
             sums[j] = lax.fori_loop(0, share // tile, block, sums[j])
         copy = pltpu.make_async_copy(update.at[:, at], out_hbm.at[:, at], out_sem.at[ch])
@@ -323,8 +345,8 @@
             stage_update(t - 3)
 
     for j in range(experts_here):
-        norms[d, j : j + 1, :] = jnp.sum(sums[j][0], axis=0, keepdims=True)
-        norms[d, experts_here + j : experts_here + j + 1, :] = jnp.sum(sums[j][1], axis=0, keepdims=True)
+        norms[d, j : j + 1, :] = jnp.sum(weight_sums[j], axis=0, keepdims=True)
+        norms[d, experts_here + j : experts_here + j + 1, :] = jnp.sum(sums[j], axis=0, keepdims=True)
     n_copies = []
     for i, flip in enumerate(flips):
         copy = pltpu.make_async_remote_copy(
@@ -394,6 +416,9 @@
             pltpu.VMEM((n_dp, share * local_rows // LANES, LANES), half_type),
             pltpu.VMEM((experts_here * share, n_dp * local_rows), half_type),
             pltpu.VMEM((experts_here * share, cols), jnp.float32),
+            pltpu.VMEM((experts_here * share, width), jnp.float32),
+            pltpu.VMEM((experts_here * share, width), jnp.float32),
+            pltpu.VMEM((experts_here * share, width), jnp.float32),
             pltpu.VMEM((experts_here * share, width), half_type),
             pltpu.VMEM((n_dp, 2 * experts_here, LANES), jnp.float32),
             dma((5,)),

time: 31 us -> 30.2 us (0.974)
  Pallas kernels: 28.5 us -> 27.7 us
    pallas_call x1, Pallas kernels: 28.5 us -> 27.7 us  [fused(): pl.pallas_call(functools.partial(fused_kernel, n_expert, CHUNKS), out_sha...]
where the time goes in v3:
time: 30.2 us; the launch traced here: 30 us
  Pallas kernels  27.7 us (92%)
  other arithmetic  2.3 us (8%)
    pallas_call x1, Pallas kernels, fused(): pl.pallas_call(functools.partial(fused_kernel, n_expert, CHUNKS), out_sha...  27.7 us
    convert_element_type x1, other arithmetic, fused(): return fresh.astype(master_weight.dtype)  2.3 us

profile of v3, /device:TPU:0, one launch (start us, length us, event | category | flops | bytes accessed | tf_op | source)
XLA Modules:
  0.0 30.0 jit_solution(6963828228168010102)
XLA Ops:
  0.0 0.0 copy-start
  0.0 27.7 %shard_map.82 = (bf16[192,2048]{1,0:T(8,128)(2,1)}, f32[2,2048]{1,0:T(2,128)}) custom-call(s32[1,8,8]{2,1,0:T(8,128)} %token_ref.1, s32[1,8]{1,0:T(1,128)} %count_ref.1, f32[1,64]{1,0:T(1,128)} %mix_ref.1, bf16[128,2048]{1,0:T(8,128)(2,1)} %grad_hbm.1, bf16[64,768]{1,0:T(8,128)(2,1)} %hidden_hbm.1, bf16[2,96,2048]{2,1,0:T(8,128)(2,1)} %weight_hbm.1, ...), custom_call_target="tpu_custom_call" | custom-call | tf_op jit(solution)/shard_map/pallas_call | solution.py:394
  27.7 0.0 copy-done
  27.7 2.3 %fusion.1 = bf16[2,96,2048]{2,1,0:T(8,128)(2,1)} fusion(bf16[2,96,2048]{2,1,0:T(8,128)(2,1)} %bitcast.2, bf16[2,96,2048]{2,1,0:T(8,128)(2,1)S(1)} %copy-done, f32[2,2048]{1,0:T(2,128)} %get-tuple-element.7), kind=kLoop, calls=%fused_computation.2 | loop fusion | flops 1966080 | bytes 2375680 | tf_op jit(solution)/shard_map/convert_element_type | solution.py:439
Async XLA Ops:
  0.0 27.7 %copy-start = (bf16[2,96,2048]{2,1,0:T(8,128)(2,1)S(1)}, bf16[2,96,2048]{2,1,0:T(8,128)(2,1)}, u32[]{:S(2)}) copy-start(bf16[2,96,2048]{2,1,0:T(8,128)(2,1)} %weight_hbm.1) | copy-start | bytes 2359300

commit v4 on v3

--- a/solution.py
+++ b/solution.py
@@ -35,9 +35,9 @@
 def fused_kernel(
     n_expert,
     chunks,
-    token_ref,
-    count_ref,
-    mix_ref,
+    token_hbm,
+    count_hbm,
+    mix_hbm,
     grad_hbm,
     hidden_hbm,
     weight_hbm,
@@ -45,6 +45,9 @@
     second_hbm,
     out_hbm,
     scale_ref,
+    token_ref,
+    count_ref,
+    mix_ref,
     grad,
     hidden,
     weight,
@@ -107,15 +110,19 @@
                 (weight_hbm, weight),
                 (first_hbm, first),
                 (second_hbm, second),
+                (count_hbm, count_ref),
+                (mix_hbm, mix_ref),
+                (token_hbm, token_ref),
             ]
         )
     ]
-    loads[1].start()
-    loads[0].start()
+    for i in (7, 1, 0, 5, 6):
+        loads[i].start()
 
     tokens = grad.shape[0]
     lane = lax.broadcasted_iota(jnp.int32, (8, tokens), 1)
     sub = lax.broadcasted_iota(jnp.int32, (8, tokens), 0)
+    loads[7].wait()
     blocks = []
     for base in range(0, local_rows, 8):
         want = jnp.zeros((8, tokens), jnp.int32)
@@ -125,7 +132,7 @@
         blocks.append(jnp.where(want == lane, 1.0, 0.0))
     onehot = jnp.concatenate(blocks, axis=0).astype(jnp.bfloat16)
     loads[1].wait()
-    for copy in loads[2:]:
+    for copy in loads[2:5]:
         copy.start()
     z_copies = []
     for ch in range(chunks):
@@ -208,6 +215,8 @@
         slot = lax.broadcasted_iota(jnp.int32, (1, LANES), 1) % local_rows
         source = (slot // slots + e) % n_expert * slots + slot % slots
         row_id = lax.broadcasted_iota(jnp.int32, (local_rows, LANES), 0)
+        loads[5].wait()
+        loads[6].wait()
         mix_rows = mix_column(mix_ref, count_ref, local_rows, capacity)
         placed = jnp.where(row_id == source, mix_rows, 0.0).astype(jnp.bfloat16)
         loads[0].wait()
@@ -285,7 +294,7 @@
     sums = [zero for _ in range(experts_here)]
 
     def stage_known():
-        for copy in loads[2:]:
+        for copy in loads[2:5]:
             copy.wait()
         for j in range(experts_here):
 
@@ -397,14 +406,12 @@
             jax.ShapeDtypeStruct((experts_here * share, width), half_type),
             jax.ShapeDtypeStruct((experts_here, width), jnp.float32),
         ),
-        in_specs=[
-            pl.BlockSpec(memory_space=pltpu.SMEM),
-            pl.BlockSpec(memory_space=pltpu.SMEM),
-            pl.BlockSpec(memory_space=pltpu.VMEM),
-        ]
-        + [anywhere] * 5,
+        in_specs=[pl.BlockSpec(memory_space=pltpu.HBM)] * 8,
         out_specs=(anywhere, pl.BlockSpec(memory_space=pltpu.VMEM)),
         scratch_shapes=[
+            pltpu.SMEM(slot_token.shape, slot_token.dtype),
+            pltpu.SMEM(counts.shape, counts.dtype),
+            pltpu.VMEM(slot_weight.shape, slot_weight.dtype),
             pltpu.VMEM(grad_out.shape, half_type),
             pltpu.VMEM(hidden.shape, half_type),
             pltpu.VMEM(master_weight.shape, half_type),
@@ -421,7 +428,7 @@
             pltpu.VMEM((experts_here * share, width), jnp.float32),
             pltpu.VMEM((experts_here * share, width), half_type),
             pltpu.VMEM((n_dp, 2 * experts_here, LANES), jnp.float32),
-            dma((5,)),
+            dma((8,)),
             dma((CHUNKS,)),
             dma((CHUNKS, n_expert - 1)),
             dma((CHUNKS, n_expert - 1)),
@@ -432,7 +439,7 @@
             dma((n_dp - 1,)),
             dma((n_dp - 1,)),
         ],
-        compiler_params=pltpu.CompilerParams(collective_id=0, has_side_effects=True),
+        compiler_params=pltpu.CompilerParams(collective_id=0, has_side_effects=True, vmem_limit_bytes=32 * 2**20),
     )(slot_token, counts, slot_weight, grad_out, hidden, master_weight, moment1, moment2)
     update = update.reshape(master_weight.shape).astype(jnp.float32)
     fresh = master_weight.astype(jnp.float32) - scale[:, None, :] * update

time: 30.2 us -> 35.1 us (1.16)
  local copies, waits for them, and re-layouts: 0.01 us -> 7.33 us
  Pallas kernels: 27.7 us -> 26.3 us
  other arithmetic: 2.3 us -> 1.16 us
    unnamed x2 -> x16, local copies, waits for them, and re-layouts: 0.01 us -> 7.33 us
    pallas_call x1, Pallas kernels: 27.7 us -> 26.3 us  [fused(): pl.pallas_call(functools.partial(fused_kernel, n_expert, CHUNKS), out_sha...]
    convert_element_type x1, other arithmetic: 2.3 us -> 1.16 us  [fused(): return fresh.astype(master_weight.dtype)]
where the time goes in v4:
time: 35.1 us; the launch traced here: 34.8 us
  Pallas kernels  26.3 us (75%)
  local copies, waits for them, and re-layouts  7.33 us (21%)
  other arithmetic  1.16 us (3%)
    pallas_call x1, Pallas kernels, fused(): pl.pallas_call(functools.partial(fused_kernel, n_expert, CHUNKS), out_sha...  26.3 us
    unnamed x16, local copies, waits for them, and re-layouts  7.33 us
    convert_element_type x1, other arithmetic, fused(): return fresh.astype(master_weight.dtype)  1.16 us

profile of v4, /device:TPU:0, one launch (start us, length us, event | category | flops | bytes accessed | tf_op | source)
XLA Modules:
  0.0 34.8 jit_solution(10752413875671281564)
XLA Ops:
  0.0 0.0 copy-start
  0.0 1.1 %copy-done = bf16[2,96,2048]{2,1,0:T(8,128)(2,1)S(1)} copy-done((bf16[2,96,2048]{2,1,0:T(8,128)(2,1)S(1)}, bf16[2,96,2048]{2,1,0:T(8,128)(2,1)}, u32[]{:S(2)}) %copy-start) | copy-done | bytes 786456
  1.1 0.0 copy-start.1
  1.1 1.1 %copy-done.1 = bf16[2,96,2048]{2,1,0:T(8,128)(2,1)S(1)} copy-done((bf16[2,96,2048]{2,1,0:T(8,128)(2,1)S(1)}, bf16[2,96,2048]{2,1,0:T(8,128)(2,1)}, u32[]{:S(2)}) %copy-start.1) | copy-done | bytes 786456
  2.3 0.0 copy-start.2
  2.3 1.1 %copy-done.2 = bf16[2,96,2048]{2,1,0:T(8,128)(2,1)S(1)} copy-done((bf16[2,96,2048]{2,1,0:T(8,128)(2,1)S(1)}, bf16[2,96,2048]{2,1,0:T(8,128)(2,1)}, u32[]{:S(2)}) %copy-start.2) | copy-done | bytes 786456
  3.4 0.0 copy-start.3
  3.4 1.0 %copy-done.3 = bf16[128,2048]{1,0:T(8,128)(2,1)S(1)} copy-done((bf16[128,2048]{1,0:T(8,128)(2,1)S(1)}, bf16[128,2048]{1,0:T(8,128)(2,1)}, u32[]{:S(2)}) %copy-start.3) | copy-done | bytes 524312
  4.4 0.0 copy-start.4
  4.4 0.9 %copy-done.4 = bf16[64,768]{1,0:T(8,128)(2,1)S(1)} copy-done((bf16[64,768]{1,0:T(8,128)(2,1)S(1)}, bf16[64,768]{1,0:T(8,128)(2,1)}, u32[]{:S(2)}) %copy-start.4) | copy-done | bytes 98328
  5.3 0.0 copy-start.5
  5.3 0.7 %copy-done.5 = s32[1,8,8]{2,1,0:T(8,128)S(1)} copy-done((s32[1,8,8]{2,1,0:T(8,128)S(1)}, s32[1,8,8]{2,1,0:T(8,128)}, u32[]{:S(2)}) %copy-start.5) | copy-done | bytes 280
  6.0 0.0 copy-start.6
  6.0 0.7 %copy-done.6 = s32[1,8]{1,0:T(1,128)S(1)} copy-done((s32[1,8]{1,0:T(1,128)S(1)}, s32[1,8]{1,0:T(1,128)}, u32[]{:S(2)}) %copy-start.6) | copy-done | bytes 56
  6.7 0.0 copy-start.7
  6.7 0.7 %copy-done.7 = f32[1,64]{1,0:T(1,128)S(1)} copy-done((f32[1,64]{1,0:T(1,128)S(1)}, f32[1,64]{1,0:T(1,128)}, u32[]{:S(2)}) %copy-start.7) | copy-done | bytes 280
  7.3 26.3 %shard_map.82 = (bf16[192,2048]{1,0:T(8,128)(2,1)S(1)}, f32[2,2048]{1,0:T(2,128)S(1)}) custom-call(s32[1,8,8]{2,1,0:T(8,128)S(1)} %copy-done.5, s32[1,8]{1,0:T(1,128)S(1)} %copy-done.6, f32[1,64]{1,0:T(1,128)S(1)} %copy-done.7, bf16[128,2048]{1,0:T(8,128)(2,1)S(1)} %copy-done.3, bf16[64,768]{1,0:T(8,128)(2,1)S(1)} %copy-done.4, ...), custom_call_target="tpu_custom_call" | custom-call | tf_op jit(solution)/shard_map/pallas_call | solution.py:403
  33.6 1.2 %fusion.1 = bf16[2,96,2048]{2,1,0:T(8,128)(2,1)} fusion(bf16[2,96,2048]{2,1,0:T(8,128)(2,1)S(1)} %bitcast.2, bf16[2,96,2048]{2,1,0:T(8,128)(2,1)S(1)} %copy-done, f32[2,2048]{1,0:T(2,128)S(1)} %get-tuple-element.7), kind=kLoop, calls=%fused_computation.2 | loop fusion | flops 1966080 | bytes 2375680 | tf_op jit(solution)/shard_map/convert_element_type | solution.py:446
Async XLA Ops:
  0.0 1.1 %copy-start = (bf16[2,96,2048]{2,1,0:T(8,128)(2,1)S(1)}, bf16[2,96,2048]{2,1,0:T(8,128)(2,1)}, u32[]{:S(2)}) copy-start(bf16[2,96,2048]{2,1,0:T(8,128)(2,1)} %weight_hbm.1) | copy-start | bytes 2359300
  1.1 1.1 %copy-start.1 = (bf16[2,96,2048]{2,1,0:T(8,128)(2,1)S(1)}, bf16[2,96,2048]{2,1,0:T(8,128)(2,1)}, u32[]{:S(2)}) copy-start(bf16[2,96,2048]{2,1,0:T(8,128)(2,1)} %first_hbm.1) | copy-start | bytes 2359300
  2.3 1.1 %copy-start.2 = (bf16[2,96,2048]{2,1,0:T(8,128)(2,1)S(1)}, bf16[2,96,2048]{2,1,0:T(8,128)(2,1)}, u32[]{:S(2)}) copy-start(bf16[2,96,2048]{2,1,0:T(8,128)(2,1)} %second_hbm.1) | copy-start | bytes 2359300
  3.4 1.0 %copy-start.3 = (bf16[128,2048]{1,0:T(8,128)(2,1)S(1)}, bf16[128,2048]{1,0:T(8,128)(2,1)}, u32[]{:S(2)}) copy-start(bf16[128,2048]{1,0:T(8,128)(2,1)} %grad_hbm.1) | copy-start | bytes 1572868
  4.4 0.9 %copy-start.4 = (bf16[64,768]{1,0:T(8,128)(2,1)S(1)}, bf16[64,768]{1,0:T(8,128)(2,1)}, u32[]{:S(2)}) copy-start(bf16[64,768]{1,0:T(8,128)(2,1)} %hidden_hbm.1) | copy-start | bytes 294916
  5.3 0.7 %copy-start.5 = (s32[1,8,8]{2,1,0:T(8,128)S(1)}, s32[1,8,8]{2,1,0:T(8,128)}, u32[]{:S(2)}) copy-start(s32[1,8,8]{2,1,0:T(8,128)} %token_hbm.1) | copy-start | bytes 772
  6.0 0.7 %copy-start.6 = (s32[1,8]{1,0:T(1,128)S(1)}, s32[1,8]{1,0:T(1,128)}, u32[]{:S(2)}) copy-start(s32[1,8]{1,0:T(1,128)} %count_hbm.1) | copy-start | bytes 100
  6.7 0.7 %copy-start.7 = (f32[1,64]{1,0:T(1,128)S(1)}, f32[1,64]{1,0:T(1,128)}, u32[]{:S(2)}) copy-start(f32[1,64]{1,0:T(1,128)} %mix_hbm.1) | copy-start | bytes 772

commit v5 on v4

--- a/solution.py
+++ b/solution.py
@@ -406,7 +406,7 @@
             jax.ShapeDtypeStruct((experts_here * share, width), half_type),
             jax.ShapeDtypeStruct((experts_here, width), jnp.float32),
         ),
-        in_specs=[pl.BlockSpec(memory_space=pltpu.HBM)] * 8,
+        in_specs=[anywhere] * 8,
         out_specs=(anywhere, pl.BlockSpec(memory_space=pltpu.VMEM)),
         scratch_shapes=[
             pltpu.SMEM(slot_token.shape, slot_token.dtype),
@@ -439,7 +439,7 @@
             dma((n_dp - 1,)),
             dma((n_dp - 1,)),
         ],
-        compiler_params=pltpu.CompilerParams(collective_id=0, has_side_effects=True, vmem_limit_bytes=32 * 2**20),
+        compiler_params=pltpu.CompilerParams(collective_id=0, has_side_effects=True),
     )(slot_token, counts, slot_weight, grad_out, hidden, master_weight, moment1, moment2)
     update = update.reshape(master_weight.shape).astype(jnp.float32)
     fresh = master_weight.astype(jnp.float32) - scale[:, None, :] * update

time: 35.1 us -> 29.3 us (0.83)
  local copies, waits for them, and re-layouts: 7.33 us -> 0.01 us
  other arithmetic: 1.16 us -> 2.3 us
  Pallas kernels: 26.3 us -> 26.8 us
    unnamed x16 -> x2, local copies, waits for them, and re-layouts: 7.33 us -> 0.01 us
    convert_element_type x1, other arithmetic: 1.16 us -> 2.3 us  [fused(): return fresh.astype(master_weight.dtype)]
    pallas_call x1, Pallas kernels: 26.3 us -> 26.8 us  [fused(): pl.pallas_call(functools.partial(fused_kernel, n_expert, CHUNKS), out_sha...]
where the time goes in v5:
time: 29.3 us; the launch traced here: 29.1 us
  Pallas kernels  26.8 us (91%)
  other arithmetic  2.3 us (8%)
    pallas_call x1, Pallas kernels, fused(): pl.pallas_call(functools.partial(fused_kernel, n_expert, CHUNKS), out_sha...  26.8 us
    convert_element_type x1, other arithmetic, fused(): return fresh.astype(master_weight.dtype)  2.3 us

profile of v5, /device:TPU:0, one launch (start us, length us, event | category | flops | bytes accessed | tf_op | source)
XLA Modules:
  0.0 29.1 jit_solution(3422109610814808568)
XLA Ops:
  0.0 0.0 copy-start
  0.0 26.8 %shard_map.82 = (bf16[192,2048]{1,0:T(8,128)(2,1)}, f32[2,2048]{1,0:T(2,128)}) custom-call(s32[1,8,8]{2,1,0:T(8,128)} %token_hbm.1, s32[1,8]{1,0:T(1,128)} %count_hbm.1, f32[1,64]{1,0:T(1,128)} %mix_hbm.1, bf16[128,2048]{1,0:T(8,128)(2,1)} %grad_hbm.1, bf16[64,768]{1,0:T(8,128)(2,1)} %hidden_hbm.1, bf16[2,96,2048]{2,1,0:T(8,128)(2,1)} %weight_hbm.1, ...), custom_call_target="tpu_custom_call" | custom-call | tf_op jit(solution)/shard_map/pallas_call | solution.py:403
  26.8 0.0 copy-done
  26.8 2.3 %fusion.1 = bf16[2,96,2048]{2,1,0:T(8,128)(2,1)} fusion(bf16[2,96,2048]{2,1,0:T(8,128)(2,1)} %bitcast.2, bf16[2,96,2048]{2,1,0:T(8,128)(2,1)S(1)} %copy-done, f32[2,2048]{1,0:T(2,128)} %get-tuple-element.7), kind=kLoop, calls=%fused_computation.2 | loop fusion | flops 1966080 | bytes 2375680 | tf_op jit(solution)/shard_map/convert_element_type | solution.py:446
Async XLA Ops:
  0.0 26.8 %copy-start = (bf16[2,96,2048]{2,1,0:T(8,128)(2,1)S(1)}, bf16[2,96,2048]{2,1,0:T(8,128)(2,1)}, u32[]{:S(2)}) copy-start(bf16[2,96,2048]{2,1,0:T(8,128)(2,1)} %weight_hbm.1) | copy-start | bytes 2359300

commit v6 on v5

--- a/solution.py
+++ b/solution.py
@@ -43,7 +43,7 @@
     weight_hbm,
     first_hbm,
     second_hbm,
-    out_hbm,
+    update,
     scale_ref,
     token_ref,
     count_ref,
@@ -62,10 +62,8 @@
     known_w,
     known_m,
     known_v,
-    update,
     norms,
     load_sem,
-    out_sem,
     z_send,
     z_recv,
     p_send,
@@ -312,7 +310,6 @@
 
             weight_sums[j] = lax.fori_loop(0, share // tile, block, weight_sums[j])
 
-    outs = []
 
     def stage_update(piece):
         p = plane[piece]
@@ -338,9 +335,6 @@
                 return carry + fold(u * u)
 
             sums[j] = lax.fori_loop(0, share // tile, block, sums[j])
-        copy = pltpu.make_async_copy(update.at[:, at], out_hbm.at[:, at], out_sem.at[ch])
-        copy.start()
-        outs.append(copy)
 
     pieces = chunks + 1
     for t in range(pieces + 3):
@@ -387,8 +381,6 @@
         scale_ref[j : j + 1, :] = jnp.broadcast_to(learn_rate * ratio, (1, width))
     for copy in n_copies:
         copy.wait_send()
-    for copy in outs:
-        copy.wait()
 
 
 def fused(n_expert, n_dp, grad_out, slot_token, hidden, slot_weight, counts, master_weight, moment1, moment2):
@@ -403,11 +395,11 @@
     update, scale = pl.pallas_call(
         functools.partial(fused_kernel, n_expert, CHUNKS),
         out_shape=(
-            jax.ShapeDtypeStruct((experts_here * share, width), half_type),
-            jax.ShapeDtypeStruct((experts_here, width), jnp.float32),
+            pltpu.VMEM((experts_here * share, width), half_type),
+            pltpu.VMEM((experts_here, width), jnp.float32),
         ),
         in_specs=[anywhere] * 8,
-        out_specs=(anywhere, pl.BlockSpec(memory_space=pltpu.VMEM)),
+        out_specs=(pl.BlockSpec(memory_space=pltpu.VMEM),) * 2,
         scratch_shapes=[
             pltpu.SMEM(slot_token.shape, slot_token.dtype),
             pltpu.SMEM(counts.shape, counts.dtype),
@@ -426,10 +418,8 @@
             pltpu.VMEM((experts_here * share, width), jnp.float32),
             pltpu.VMEM((experts_here * share, width), jnp.float32),
             pltpu.VMEM((experts_here * share, width), jnp.float32),
-            pltpu.VMEM((experts_here * share, width), half_type),
             pltpu.VMEM((n_dp, 2 * experts_here, LANES), jnp.float32),
             dma((8,)),
-            dma((CHUNKS,)),
             dma((CHUNKS, n_expert - 1)),
             dma((CHUNKS, n_expert - 1)),
             dma((CHUNKS + 1, 9)),

time: 29.3 us -> 27.5 us (0.939)
  other arithmetic: 2.3 us -> 1.16 us
  Pallas kernels: 26.8 us -> 26.2 us
    convert_element_type x1, other arithmetic: 2.3 us -> 1.16 us  [fused(): return fresh.astype(master_weight.dtype)]
    pallas_call x1, Pallas kernels: 26.8 us -> 26.2 us  [fused(): pl.pallas_call(functools.partial(fused_kernel, n_expert, CHUNKS), out_sha...]
where the time goes in v6:
time: 27.5 us; the launch traced here: 27.4 us
  Pallas kernels  26.2 us (95%)
  other arithmetic  1.16 us (4%)
    pallas_call x1, Pallas kernels, fused(): pl.pallas_call(functools.partial(fused_kernel, n_expert, CHUNKS), out_sha...  26.2 us
    convert_element_type x1, other arithmetic, fused(): return fresh.astype(master_weight.dtype)  1.16 us

profile of v6, /device:TPU:0, one launch (start us, length us, event | category | flops | bytes accessed | tf_op | source)
XLA Modules:
  0.0 27.4 jit_solution(5244249714513275526)
XLA Ops:
  0.0 0.0 copy-start
  0.0 26.2 %shard_map.82 = (bf16[192,2048]{1,0:T(8,128)(2,1)S(1)}, f32[2,2048]{1,0:T(2,128)S(1)}) custom-call(s32[1,8,8]{2,1,0:T(8,128)} %token_hbm.1, s32[1,8]{1,0:T(1,128)} %count_hbm.1, f32[1,64]{1,0:T(1,128)} %mix_hbm.1, bf16[128,2048]{1,0:T(8,128)(2,1)} %grad_hbm.1, bf16[64,768]{1,0:T(8,128)(2,1)} %hidden_hbm.1, bf16[2,96,2048]{2,1,0:T(8,128)(2,1)} %weight_hbm.1, ...), custom_call_target="tpu_custom_call" | custom-call | tf_op jit(solution)/shard_map/pallas_call | solution.py:395
  26.2 0.0 copy-done
  26.2 1.2 %fusion.1 = bf16[2,96,2048]{2,1,0:T(8,128)(2,1)} fusion(bf16[2,96,2048]{2,1,0:T(8,128)(2,1)S(1)} %bitcast.2, bf16[2,96,2048]{2,1,0:T(8,128)(2,1)S(1)} %copy-done, f32[2,2048]{1,0:T(2,128)S(1)} %get-tuple-element.7), kind=kLoop, calls=%fused_computation.2 | loop fusion | flops 1966080 | bytes 2375680 | tf_op jit(solution)/shard_map/convert_element_type | solution.py:436
Async XLA Ops:
  0.0 26.2 %copy-start = (bf16[2,96,2048]{2,1,0:T(8,128)(2,1)S(1)}, bf16[2,96,2048]{2,1,0:T(8,128)(2,1)}, u32[]{:S(2)}) copy-start(bf16[2,96,2048]{2,1,0:T(8,128)(2,1)} %weight_hbm.1) | copy-start | bytes 2359300
